TPU v7x, 128 devices: a whole 4x4x4 slice. The times are simulated.
128 devices in a mesh: row: 16 (over y, x), col: 8 (over z, core).
Axes of the slice: x: 4, y: 4, z: 4, core: 2. Of those that a mesh axis runs over, the one named last changes fastest.
Arguments:
- orbitals: float32 [32768, 1024], P('row', 'col'), may hold values from -6 to 6
- point_index: int32 [8192], replicated, may hold values from 0 to 32767, as said below
- coulomb: float32 [8192, 8192], P('row', 'col'), may hold values from -0.001953125 to 0.001953125
- fitting: float32 [32768, 8192], P('row', 'col'), may hold values from -0.0625 to 0.0625
Outputs:
- exchange_out: float32 [32768, 1024], P('row', 'col')
Inputs may be any that keep to these rules, and one draw needn't show every extreme that they name: `point_index`: indices are distinct. Grid index g lies in slab g // 2048. Of the 512 consecutive points of each row panel, at most 64 lie in one slab, and in every panel exactly 64 lie in one slab.
All inputs are finite; a program needn't handle non-finite values.
Results may differ from a plain program's by a relative error of at most 0.00012.
Values sent between devices are 32-bit elements; how exact they have to be, the bound alone decides.
No kernel may reach another device: no remote copies, remote signals or barrier semaphores. Data moves between devices by JAX's collectives and lax.ppermute only.
A program may use at most 64 MiB of HBM per device.

v0:
```python
import jax
import jax.numpy as jnp
from jax import lax
from jax.sharding import PartitionSpec as P


def per_device(orbitals, point_index, coulomb, fitting):
    row_count = lax.axis_size("row")
    slab_rows = orbitals.shape[0]
    band_cols = orbitals.shape[1]
    total_points = point_index.shape[0]
    per_panel = total_points // row_count
    slot_count = 2 * per_panel // row_count
    my_row = lax.axis_index("row")
    my_col = lax.axis_index("col")
    owner = point_index // slab_rows
    local_row = point_index - owner * slab_rows
    owner_grid = owner.reshape(row_count, per_panel)
    local_grid = local_row.reshape(row_count, per_panel)
    matches = (owner_grid[:, :, None] == jnp.arange(row_count)[None, None, :]).astype(jnp.int32)
    ranking = jnp.cumsum(matches, axis=1) - 1
    slot_grid = jnp.sum(jnp.where(matches > 0, ranking, 0), axis=2)
    mine = owner_grid == my_row
    chosen = mine[:, :, None] & (slot_grid[:, :, None] == jnp.arange(slot_count)[None, None, :])
    source_row = jnp.sum(jnp.where(chosen, local_grid[:, :, None], 0), axis=1)
    valid = jnp.any(chosen, axis=1)
    outgoing = jnp.where(valid[:, :, None], orbitals[source_row], 0.0)
    received = lax.all_to_all(outgoing, "row", split_axis=0, concat_axis=0, tiled=True)
    flattened = received.reshape(row_count * slot_count, band_cols)
    owner_mine = lax.dynamic_slice_in_dim(owner_grid, my_row, 1, 0)[0]
    slot_mine = lax.dynamic_slice_in_dim(slot_grid, my_row, 1, 0)[0]
    panel_strip = flattened[owner_mine * slot_count + slot_mine]
    panel_full = lax.all_gather(panel_strip, "col", axis=1, tiled=True)
    strip_all = lax.all_gather(panel_strip, "row", axis=0, tiled=True)
    column_full = lax.all_to_all(strip_all, "col", split_axis=0, concat_axis=1, tiled=True)
    pair = jnp.dot(
        panel_full,
        column_full.T,
        precision=lax.Precision.HIGHEST,
        preferred_element_type=jnp.float32,
    )
    partial_value = jnp.dot(
        coulomb * pair,
        column_full,
        precision=lax.Precision.HIGHEST,
        preferred_element_type=jnp.float32,
    )
    summed = lax.psum(partial_value, "col")
    weight_strip = lax.dynamic_slice_in_dim(summed, my_col * band_cols, band_cols, 1)
    weight_all = lax.all_gather(weight_strip, "row", axis=0, tiled=True)
    weight_column = lax.all_to_all(weight_all, "col", split_axis=0, concat_axis=1, tiled=True)
    term = -jnp.dot(
        fitting, weight_column, precision=lax.Precision.HIGHEST, preferred_element_type=jnp.float32
    )
    return lax.psum_scatter(term, "col", scatter_dimension=1, tiled=True)


def solution(mesh):
    in_specs = (P("row", "col"), P(), P("row", "col"), P("row", "col"))
    out_specs = P("row", "col")
    return jax.shard_map(
        per_device, mesh=mesh, in_specs=in_specs, out_specs=out_specs, check_vma=False
    )
```

profile of v0, /device:TPU:1, one launch (start us, length us, event | category | flops | bytes accessed | tf_op | source)
XLA Modules:
  0.0 455.0 jit_solution(17053227646644260959)
XLA Ops:
  6.5 0.9 add_select_fusion
  7.5 18.1 %reduce-window.6 = s32[16,16,4,128]{3,1,2,0:T(8,128)S(1)} reduce-window(s32[16,16,4,128]{3,1,2,0:T(8,128)S(1)} %fusion.6, s32[]{:T(128)} %constant.16.clone.1), window={size=1x1x1x128 pad=0_0x0_0x0_0x127_0}, to_apply=%region_0.1 | reduce-window | flops 16646144 | bytes 1048580 | tf_op jit(solution)/shard_map/reduce-window
  27.1 0.5 select_reduce_fusion
  27.7 2.8 gather_fusion
  30.6 1.0 broadcast_select_fusion
  31.6 7.6 %all-to-all-start = ((f32[16,64,128]{2,1,0:T(8,128)}), f32[16,64,128]{2,1,0:T(8,128)S(1)}, u32[]{:S(2)}, u32[]{:S(2)}) async-start(f32[16,64,128]{2,1,0:T(8,128)} %broadcast_select_fusion), calls=%async_computation | async-start | bytes 1048576 | tf_op jit(solution)/shard_map/all_to_all | solution.py:28
  39.2 10.3 %all-to-all-done = f32[16,64,128]{2,1,0:T(8,128)S(1)} async-done(((f32[16,64,128]{2,1,0:T(8,128)}), f32[16,64,128]{2,1,0:T(8,128)S(1)}, u32[]{:S(2)}, u32[]{:S(2)}) %all-to-all-start) | async-done | bytes 524320 | tf_op jit(solution)/shard_map/all_to_all | solution.py:28
  49.6 1.6 gather_fusion.1
  51.3 0.7 all-gather.8.cloned.1.call-update
  52.0 50.4 %all-gather.10.cloned.1.call-done = f32[8192,128]{1,0:T(8,128)} async-done(((f32[512,128]{1,0:T(8,128)}), f32[8192,128]{1,0:T(8,128)}) %all-gather.10.cloned.1.call-update) | async-done | bytes 4194320 | tf_op jit(solution)/shard_map/all_gather | solution.py:34
  102.4 5.4 %copy.15 = f32[8,1024,128]{1,2,0:T(8,128)} copy(f32[8,1024,128]{2,1,0:T(8,128)} %bitcast.44) | data formatting | bytes 8388608 | tf_op jit(solution)/shard_map/all_to_all | solution.py:35
  107.7 5.3 %all-to-all-start.1 = ((f32[8,1024,128]{1,2,0:T(8,128)}), f32[8,1024,128]{1,2,0:T(8,128)}, u32[]{:S(2)}, u32[]{:S(2)}) async-start(f32[8,1024,128]{1,2,0:T(8,128)} %copy.15), calls=%async_computation.1 | async-start | bytes 8388608 | tf_op jit(solution)/shard_map/all_to_all | solution.py:35
  113.0 31.5 %all-gather.8.cloned.1.call-done = f32[512,1024]{1,0:T(8,128)} async-done(((f32[512,128]{1,0:T(8,128)}), f32[512,1024]{1,0:T(8,128)}) %all-gather.8.cloned.1.call-update) | async-done | bytes 2097168 | tf_op jit(solution)/shard_map/all_gather | solution.py:33
  144.5 25.7 %all-to-all-done.1 = f32[8,1024,128]{1,2,0:T(8,128)} async-done(((f32[8,1024,128]{1,2,0:T(8,128)}), f32[8,1024,128]{1,2,0:T(8,128)}, u32[]{:S(2)}, u32[]{:S(2)}) %all-to-all-start.1) | async-done | bytes 4194336 | tf_op jit(solution)/shard_map/all_to_all | solution.py:35
  170.2 9.8 %fusion.11 = f32[512,1024]{1,0:T(8,128)S(1)} fusion(f32[512,1024]{1,0:T(8,128)} %all-gather.8.cloned.1.call-done, f32[1024,1024]{0,1:T(8,128)} %bitcast.10), kind=kOutput, calls=%fused_computation.34 | convolution fusion | flops 6442450944 | bytes 8388608 | tf_op jit(solution)/shard_map/dot_general | solution.py:36
  180.0 9.8 %fusion = f32[512,1024]{1,0:T(8,128)} fusion(f32[1024,1024]{0,1:T(8,128)} %bitcast.10, f32[512,1024]{1,0:T(8,128)S(1)} %copy-done.1, f32[512,1024]{1,0:T(8,128)S(1)} %fusion.11), kind=kOutput, calls=%fused_computation.3 | convolution fusion | flops 6442975232 | bytes 10485760 | tf_op jit(solution)/shard_map/dot_general | solution.py:42
  189.9 62.2 %all-reduce.2.cloned.1.call-done = f32[512,1024]{1,0:T(8,128)} async-done(((f32[512,1024]{1,0:T(8,128)}), f32[512,1024]{1,0:T(8,128)}) %all-reduce.2.cloned.1.call-update) | async-done | bytes 2097168 | tf_op jit(solution)/shard_map/psum | solution.py:48
  252.1 1.7 constant_dynamic-slice_fusion
  253.8 52.7 %all-gather.6.cloned.1.call-done = f32[8192,128]{1,0:T(8,128)} async-done(((f32[512,128]{1,0:T(8,128)}), f32[8192,128]{1,0:T(8,128)}) %all-gather.6.cloned.1.call-update) | async-done | bytes 4194320 | tf_op jit(solution)/shard_map/all_gather | solution.py:50
  306.5 5.4 %copy.16 = f32[8,1024,128]{1,2,0:T(8,128)} copy(f32[8,1024,128]{2,1,0:T(8,128)} %bitcast.45) | data formatting | bytes 8388608 | tf_op jit(solution)/shard_map/all_to_all | solution.py:51
  311.9 53.9 %all_to_all.43 = f32[8,1024,128]{1,2,0:T(8,128)S(1)} all-to-all(f32[8,1024,128]{1,2,0:T(8,128)} %copy.16), channel_id=1, replica_groups=mesh['row'=16,'col'=8] {'col'}, dimensions={0} | all-to-all | bytes 8388608 | tf_op jit(solution)/shard_map/all_to_all | solution.py:51
  365.8 29.9 %negate_bitcast_fusion = f32[2048,1024]{0,1:T(8,128)} fusion(f32[1024,1024]{0,1:T(8,128)S(1)} %bitcast.46, f32[2048,1024]{1,0:T(8,128)} %param.7), kind=kOutput, calls=%fused_computation.2 | convolution fusion | flops 25771900928 | bytes 20971520 | tf_op jit(solution)/shard_map/dot_general | solution.py:52
  395.7 50.2 %reduce-scatter.2.cloned.1.call-done = f32[2048,128]{0,1:T(8,128)} async-done(((f32[2048,1024]{0,1:T(8,128)}), f32[2048,128]{0,1:T(8,128)}) %reduce-scatter.2.cloned.1.call-update) | async-done | bytes 1048592 | tf_op jit(solution)/shard_map/reduce_scatter | solution.py:55
  445.9 2.5 copy.17
  (29 shorter events, 1.8 us)
Async XLA Ops:
  6.5 21.2 %copy-start = (f32[2048,128]{1,0:T(8,128)S(1)}, f32[2048,128]{1,0:T(8,128)}, u32[]{:S(2)}) copy-start(f32[2048,128]{1,0:T(8,128)} %param.4) | copy-start | bytes 3145732
  31.6 18.0 %all-to-all-start = ((f32[16,64,128]{2,1,0:T(8,128)}), f32[16,64,128]{2,1,0:T(8,128)S(1)}, u32[]{:S(2)}, u32[]{:S(2)}) async-start(f32[16,64,128]{2,1,0:T(8,128)} %broadcast_select_fusion), calls=%async_computation | async-start | bytes 1048576 | tf_op jit(solution)/shard_map/all_to_all | solution.py:28
  39.1 63.2 %all-gather.10.cloned.1.call-start = ((), (), s32[]{:S(2)}) async-start(), calls=%async_computation.8 | async-start | bytes 4456448 | tf_op jit(solution)/shard_map/all_gather | solution.py:34
  51.2 93.3 %all-gather.8.cloned.1.call-start = ((), (), s32[]{:S(2)}) async-start(), calls=%async_computation.7 | async-start | bytes 2359296 | tf_op jit(solution)/shard_map/all_gather | solution.py:33
  107.7 62.5 %all-to-all-start.1 = ((f32[8,1024,128]{1,2,0:T(8,128)}), f32[8,1024,128]{1,2,0:T(8,128)}, u32[]{:S(2)}, u32[]{:S(2)}) async-start(f32[8,1024,128]{1,2,0:T(8,128)} %copy.15), calls=%async_computation.1 | async-start | bytes 8388608 | tf_op jit(solution)/shard_map/all_to_all | solution.py:35
  113.0 139.1 %all-reduce.2.cloned.1.call-start = ((), (), s32[]{:S(2)}) async-start(), calls=%async_computation.4 | async-start | bytes 4194304 | tf_op jit(solution)/shard_map/psum | solution.py:48
  170.2 9.8 %copy-start.1 = (f32[512,1024]{1,0:T(8,128)S(1)}, f32[512,1024]{1,0:T(8,128)}, u32[]{:S(2)}) copy-start(f32[512,1024]{1,0:T(8,128)} %param.6) | copy-start | bytes 6291460
  189.8 116.7 %all-gather.6.cloned.1.call-start = ((), (), s32[]{:S(2)}) async-start(), calls=%async_computation.5 | async-start | bytes 4456448 | tf_op jit(solution)/shard_map/all_gather | solution.py:50
  253.7 192.2 %reduce-scatter.2.cloned.1.call-start = ((), (), s32[]{:S(2)}) async-start(), calls=%async_computation.6 | async-start | bytes 9437184 | tf_op jit(solution)/shard_map/reduce_scatter | solution.py:55
Sparse Core Ops, SparseCore 0:
  51.3 50.9 all-gather.9
  104.0 40.3 all-gather.7
  190.0 62.0 all-reduce.1
  254.1 52.4 all-gather.5
  395.8 50.0 reduce-scatter.1
where the time goes:
time: 456 us; the launch traced here: 455 us
  waiting for transfers between devices  284 us (62%)
  blocking collectives  53.9 us (12%)
  matrix products  49.4 us (11%)
  other arithmetic  21.4 us (5%)
  local copies, waits for them, and re-layouts  20.1 us (4%)
  between operations  13.3 us (3%)
  starting transfers between devices  13 us (3%)
    psum x1, waiting for transfers between devices, per_device(): summed = lax.psum(partial_value, 'col')  62.2 us
    all_to_all x1, blocking collectives, per_device(): lax.all_to_all(weight_all, 'col', split_axis=0, concat_axis=1, tiled=True)  53.9 us
    all_gather x1, waiting for transfers between devices, per_device(): weight_all = lax.all_gather(weight_strip, 'row', axis=0, tiled=True)  52.7 us
    all_gather x1, waiting for transfers between devices, per_device(): strip_all = lax.all_gather(panel_strip, 'row', axis=0, tiled=True)  50.4 us
    reduce_scatter x1, waiting for transfers between devices, per_device(): return lax.psum_scatter(term, 'col', scatter_dimension=1, tiled=True)  50.2 us
    all_gather x1, waiting for transfers between devices, per_device(): panel_full = lax.all_gather(panel_strip, 'col', axis=1, tiled=True)  31.5 us
    dot_general x1, matrix products, per_device(): jnp.dot(fitting, weight_column, precision=lax.Precision.HIGHEST, preferre...  29.9 us
    all_to_all x1, waiting for transfers between devices, per_device(): lax.all_to_all(strip_all, 'col', split_axis=0, concat_axis=1, tiled=True)  25.7 us
  transfers between devices with their start and end apart: 7, of which 7 were waited for; matrix products, arithmetic and copies ran while one was open for 1% of the time, Pallas kernels for 0%

commit v1 on v0

--- a/solution.py
+++ b/solution.py
@@ -45,7 +45,7 @@
         precision=lax.Precision.HIGHEST,
         preferred_element_type=jnp.float32,
     )
-    summed = lax.psum(partial_value, "col")
+    summed = jnp.sum(lax.all_gather(partial_value, "col"), axis=0)
     weight_strip = lax.dynamic_slice_in_dim(summed, my_col * band_cols, band_cols, 1)
     weight_all = lax.all_gather(weight_strip, "row", axis=0, tiled=True)
     weight_column = lax.all_to_all(weight_all, "col", split_axis=0, concat_axis=1, tiled=True)

time: 456 us -> 484 us (1.061)
  waiting for transfers between devices: 284 us -> 304 us
  other arithmetic: 21.4 us -> 29.3 us
    all_gather x0 -> x1, waiting for transfers between devices: none -> 83.6 us  [per_device(): summed = jnp.sum(lax.all_gather(partial_value, 'col'), axis=0)]
    psum x1 -> x0, waiting for transfers between devices: 62.2 us -> none  [per_device(): summed = lax.psum(partial_value, 'col')]
    reduce_sum x0 -> x1, other arithmetic: none -> 7.96 us  [per_device(): summed = jnp.sum(lax.all_gather(partial_value, 'col'), axis=0)]
where the time goes in v1:
time: 484 us; the launch traced here: 483 us
  waiting for transfers between devices  304 us (63%)
  blocking collectives  54.2 us (11%)
  matrix products  50.6 us (10%)
  other arithmetic  29.3 us (6%)
  local copies, waits for them, and re-layouts  19.2 us (4%)
  between operations  13.3 us (3%)
  starting transfers between devices  13 us (3%)
    all_gather x1, waiting for transfers between devices, per_device(): summed = jnp.sum(lax.all_gather(partial_value, 'col'), axis=0)  83.6 us
    all_to_all x1, blocking collectives, per_device(): lax.all_to_all(weight_all, 'col', split_axis=0, concat_axis=1, tiled=True)  54.2 us
    all_gather x1, waiting for transfers between devices, per_device(): weight_all = lax.all_gather(weight_strip, 'row', axis=0, tiled=True)  51.2 us
    all_gather x1, waiting for transfers between devices, per_device(): strip_all = lax.all_gather(panel_strip, 'row', axis=0, tiled=True)  50.4 us
    reduce_scatter x1, waiting for transfers between devices, per_device(): return lax.psum_scatter(term, 'col', scatter_dimension=1, tiled=True)  50.2 us
    all_gather x1, waiting for transfers between devices, per_device(): panel_full = lax.all_gather(panel_strip, 'col', axis=1, tiled=True)  31.5 us
    dot_general x1, matrix products, per_device(): jnp.dot(fitting, weight_column, precision=lax.Precision.HIGHEST, preferre...  31 us
    all_to_all x1, waiting for transfers between devices, per_device(): lax.all_to_all(strip_all, 'col', split_axis=0, concat_axis=1, tiled=True)  25.7 us
  transfers between devices with their start and end apart: 7, of which 7 were waited for; matrix products, arithmetic and copies ran while one was open for 1% of the time, Pallas kernels for 0%

profile of v1, /device:TPU:1, one launch (start us, length us, event | category | flops | bytes accessed | tf_op | source)
XLA Modules:
  0.0 483.5 jit_solution(137309192027345048)
XLA Ops:
  6.5 0.9 add_select_fusion
  7.5 18.1 %reduce-window.6 = s32[16,16,4,128]{3,1,2,0:T(8,128)S(1)} reduce-window(s32[16,16,4,128]{3,1,2,0:T(8,128)S(1)} %fusion.6, s32[]{:T(128)} %constant.16.clone.1), window={size=1x1x1x128 pad=0_0x0_0x0_0x127_0}, to_apply=%region_0.1 | reduce-window | flops 16646144 | bytes 1048580 | tf_op jit(solution)/shard_map/reduce-window
  27.7 2.8 gather_fusion
  30.6 1.0 broadcast_select_fusion
  31.6 7.6 %all-to-all-start = ((f32[16,64,128]{2,1,0:T(8,128)}), f32[16,64,128]{2,1,0:T(8,128)S(1)}, u32[]{:S(2)}, u32[]{:S(2)}) async-start(f32[16,64,128]{2,1,0:T(8,128)} %broadcast_select_fusion), calls=%async_computation | async-start | bytes 1048576 | tf_op jit(solution)/shard_map/all_to_all | solution.py:28
  39.2 10.3 %all-to-all-done = f32[16,64,128]{2,1,0:T(8,128)S(1)} async-done(((f32[16,64,128]{2,1,0:T(8,128)}), f32[16,64,128]{2,1,0:T(8,128)S(1)}, u32[]{:S(2)}, u32[]{:S(2)}) %all-to-all-start) | async-done | bytes 524320 | tf_op jit(solution)/shard_map/all_to_all | solution.py:28
  49.6 1.6 gather_fusion.1
  51.3 0.7 all-gather.10.cloned.1.call-update
  52.0 50.4 %all-gather.12.cloned.1.call-done = f32[8192,128]{1,0:T(8,128)} async-done(((f32[512,128]{1,0:T(8,128)}), f32[8192,128]{1,0:T(8,128)}) %all-gather.12.cloned.1.call-update) | async-done | bytes 4194320 | tf_op jit(solution)/shard_map/all_gather | solution.py:34
  102.4 5.4 %copy.20 = f32[8,1024,128]{1,2,0:T(8,128)} copy(f32[8,1024,128]{2,1,0:T(8,128)} %bitcast.46) | data formatting | bytes 8388608 | tf_op jit(solution)/shard_map/all_to_all | solution.py:35
  107.7 5.3 %all-to-all-start.1 = ((f32[8,1024,128]{1,2,0:T(8,128)}), f32[8,1024,128]{1,2,0:T(8,128)}, u32[]{:S(2)}, u32[]{:S(2)}) async-start(f32[8,1024,128]{1,2,0:T(8,128)} %copy.20), calls=%async_computation.1 | async-start | bytes 8388608 | tf_op jit(solution)/shard_map/all_to_all | solution.py:35
  113.0 31.5 %all-gather.10.cloned.1.call-done = f32[512,1024]{1,0:T(8,128)} async-done(((f32[512,128]{1,0:T(8,128)}), f32[512,1024]{1,0:T(8,128)}) %all-gather.10.cloned.1.call-update) | async-done | bytes 2097168 | tf_op jit(solution)/shard_map/all_gather | solution.py:33
  144.5 25.7 %all-to-all-done.1 = f32[8,1024,128]{1,2,0:T(8,128)} async-done(((f32[8,1024,128]{1,2,0:T(8,128)}), f32[8,1024,128]{1,2,0:T(8,128)}, u32[]{:S(2)}, u32[]{:S(2)}) %all-to-all-start.1) | async-done | bytes 4194336 | tf_op jit(solution)/shard_map/all_to_all | solution.py:35
  170.2 9.8 %fusion.11 = f32[512,1024]{1,0:T(8,128)S(1)} fusion(f32[512,1024]{1,0:T(8,128)} %all-gather.10.cloned.1.call-done, f32[1024,1024]{0,1:T(8,128)} %bitcast.10), kind=kOutput, calls=%fused_computation.34 | convolution fusion | flops 6442450944 | bytes 8388608 | tf_op jit(solution)/shard_map/dot_general | solution.py:36
  180.0 9.8 %fusion = f32[512,1024]{1,0:T(8,128)} fusion(f32[1024,1024]{0,1:T(8,128)} %bitcast.10, f32[512,1024]{1,0:T(8,128)S(1)} %copy-done.2, f32[512,1024]{1,0:T(8,128)S(1)} %fusion.11), kind=kOutput, calls=%fused_computation.3 | convolution fusion | flops 6442975232 | bytes 10485760 | tf_op jit(solution)/shard_map/dot_general | solution.py:42
  189.9 83.6 %all-gather.14.cloned.1.call-done = f32[4096,1024]{1,0:T(8,128)} async-done(((f32[512,1024]{1,0:T(8,128)}), f32[4096,1024]{1,0:T(8,128)}) %all-gather.14.cloned.1.call-update) | async-done | bytes 16777232 | tf_op jit(solution)/shard_map/all_gather | solution.py:48
  273.6 8.0 %reduce_sum.32 = f32[512,1024]{1,0:T(8,128)S(1)} reduce(f32[8,512,1024]{2,1,0:T(8,128)} %bitcast.43, f32[]{:T(128)} %constant.44.clone.1), dimensions={0}, to_apply=%region_5.6 | reduce | flops 3670016 | bytes 18874372 | tf_op jit(solution)/shard_map/reduce_sum | solution.py:48
  281.5 0.7 constant_dynamic-slice_fusion
  282.4 51.2 %all-gather.8.cloned.1.call-done = f32[8192,128]{1,0:T(8,128)} async-done(((f32[512,128]{1,0:T(8,128)}), f32[8192,128]{1,0:T(8,128)}) %all-gather.8.cloned.1.call-update) | async-done | bytes 4194320 | tf_op jit(solution)/shard_map/all_gather | solution.py:50
  333.6 54.2 %all_to_all.43 = f32[8,1024,128]{2,1,0:T(8,128)} all-to-all(f32[8,1024,128]{2,1,0:T(8,128)} %bitcast.47), channel_id=1, replica_groups=mesh['row'=16,'col'=8] {'col'}, dimensions={0} | all-to-all | bytes 8388608 | tf_op jit(solution)/shard_map/all_to_all | solution.py:51
  387.8 5.3 %copy.21 = f32[1024,8,128]{0,2,1:T(8,128)} copy(f32[1024,8,128]{2,0,1:T(8,128)} %bitcast.44) | data formatting | bytes 8388608 | tf_op jit(solution)/shard_map/all_to_all | solution.py:51
  393.1 31.0 %negate_bitcast_fusion = f32[2048,1024]{0,1:T(8,128)} fusion(f32[1024,1024]{0,1:T(8,128)} %bitcast.48, f32[2048,1024]{1,0:T(8,128)} %param.7), kind=kOutput, calls=%fused_computation.2 | convolution fusion | flops 25771900928 | bytes 20971520 | tf_op jit(solution)/shard_map/dot_general | solution.py:52
  424.2 50.2 %reduce-scatter.2.cloned.1.call-done = f32[2048,128]{0,1:T(8,128)} async-done(((f32[2048,1024]{0,1:T(8,128)}), f32[2048,128]{0,1:T(8,128)}) %reduce-scatter.2.cloned.1.call-update) | async-done | bytes 1048592 | tf_op jit(solution)/shard_map/reduce_scatter | solution.py:55
  474.4 2.5 copy.22
  (32 shorter events, 2.4 us)
Async XLA Ops:
  6.5 21.2 %copy-start = (f32[2048,128]{1,0:T(8,128)S(1)}, f32[2048,128]{1,0:T(8,128)}, u32[]{:S(2)}) copy-start(f32[2048,128]{1,0:T(8,128)} %param.4) | copy-start | bytes 3145732
  31.6 18.0 %all-to-all-start = ((f32[16,64,128]{2,1,0:T(8,128)}), f32[16,64,128]{2,1,0:T(8,128)S(1)}, u32[]{:S(2)}, u32[]{:S(2)}) async-start(f32[16,64,128]{2,1,0:T(8,128)} %broadcast_select_fusion), calls=%async_computation | async-start | bytes 1048576 | tf_op jit(solution)/shard_map/all_to_all | solution.py:28
  39.1 63.2 %all-gather.12.cloned.1.call-start = ((), (), s32[]{:S(2)}) async-start(), calls=%async_computation.7 | async-start | bytes 4456448 | tf_op jit(solution)/shard_map/all_gather | solution.py:34
  51.2 93.3 %all-gather.10.cloned.1.call-start = ((), (), s32[]{:S(2)}) async-start(), calls=%async_computation.6 | async-start | bytes 2359296 | tf_op jit(solution)/shard_map/all_gather | solution.py:33
  107.7 62.5 %all-to-all-start.1 = ((f32[8,1024,128]{1,2,0:T(8,128)}), f32[8,1024,128]{1,2,0:T(8,128)}, u32[]{:S(2)}, u32[]{:S(2)}) async-start(f32[8,1024,128]{1,2,0:T(8,128)} %copy.20), calls=%async_computation.1 | async-start | bytes 8388608 | tf_op jit(solution)/shard_map/all_to_all | solution.py:35
  113.0 160.6 %all-gather.14.cloned.1.call-start = ((), (), s32[]{:S(2)}) async-start(), calls=%async_computation.8 | async-start | bytes 18874368 | tf_op jit(solution)/shard_map/all_gather | solution.py:48
  170.2 9.8 %copy-start.2 = (f32[512,1024]{1,0:T(8,128)S(1)}, f32[512,1024]{1,0:T(8,128)}, u32[]{:S(2)}) copy-start(f32[512,1024]{1,0:T(8,128)} %param.6) | copy-start | bytes 6291460
  189.9 143.7 %all-gather.8.cloned.1.call-start = ((), (), s32[]{:S(2)}) async-start(), calls=%async_computation.4 | async-start | bytes 4456448 | tf_op jit(solution)/shard_map/all_gather | solution.py:50
  282.3 192.1 %reduce-scatter.2.cloned.1.call-start = ((), (), s32[]{:S(2)}) async-start(), calls=%async_computation.5 | async-start | bytes 9437184 | tf_op jit(solution)/shard_map/reduce_scatter | solution.py:55
  424.2 52.8 %copy-start.1 = (f32[2048,128]{1,0:T(8,128)S(1)}, f32[2048,128]{1,0:T(8,128)}, u32[]{:S(2)}) copy-start(f32[2048,128]{1,0:T(8,128)} %param.4) | copy-start | bytes 3145732
Sparse Core Ops, SparseCore 0:
  51.3 50.9 all-gather.11
  104.0 40.4 all-gather.9
  190.0 83.5 all-gather.13
  282.4 51.1 all-gather.7
  424.3 50.0 reduce-scatter.1
